TPU v7x, 32 devices: a whole 2x2x4 slice. The times are simulated.
32 devices in a mesh: slab: 2 (over x), pair: 8 (over z, y), quad: 2 (over core).
Axes of the slice: x: 2, y: 2, z: 4, core: 2. Of those that a mesh axis runs over, the one named last changes fastest.
Arguments:
- interferograms: float32 [64, 512, 1024], P(('pair', 'quad'), 'slab'), parts along dimension 1, may hold values from -24 to 24
- pair_epochs: int32 [2, 64], replicated, may hold values from 0 to 31, as said below
- days: int32 [32], replicated, may hold values from 0 to 732, as said below
Outputs:
- smoothed: float32 [32, 512, 1024], P(None, ('slab', 'pair'), 'quad'), parts along dimension 1
There are 2 independent parts, one for each index of `slab`. A program takes and returns all parts, laid end to end along the dimension named above; an argument that names none is the same for every part. Nothing has to cross between parts.
Inputs may be any that keep to these rules, and one draw needn't show every extreme that they name: pair_epochs[0, p] < pair_epochs[1, p] for every pair, the difference is at most 8, and every two consecutive epochs e, e + 1 form one of the pairs. days are strictly increasing, days[0] = 0, consecutive days differ by 12, 24 or 36, and the last day is always the maximum.
All inputs are finite; a program needn't handle non-finite values.
Results may differ from a plain program's by a relative error of at most 0.000071.
Values sent between devices are 32-bit elements; how exact they have to be, the bound alone decides.
No kernel may reach another device: no remote copies, remote signals or barrier semaphores. Data moves between devices by JAX's collectives and lax.ppermute only.
A program may use at most 64 MiB of HBM per device.

v0:
```python
import functools

import jax
import jax.numpy as jnp
from jax import lax
from jax.experimental import pallas as pl
from jax.experimental.pallas import tpu as pltpu
from jax.sharding import PartitionSpec as P


E = 32
TREND = 4
RADIUS = 6
SUB = 8
LANE = 128
HALO = 8
WIDE = 256
PARTS = 3
TERMS = ((0, 0), (0, 1), (1, 0), (1, 1), (0, 2), (2, 0))
HIGHEST = lax.Precision.HIGHEST
AXES = ("pair", "quad")

VMEM_LIMIT = 16 << 20


def operator_body(epochs_ref, days_ref, whole_ref, narrow_ref, basis_ref):
    epochs = epochs_ref[...]
    at = lax.broadcasted_iota(jnp.int32, (E, epochs.shape[1]), 0)
    design = ((epochs[0:1, :] <= at) & (at < epochs[1:2, :])).astype(jnp.float32)
    row = lax.broadcasted_iota(jnp.int32, (E, E), 0)
    lane = lax.broadcasted_iota(jnp.int32, (E, E), 1)
    rows = lax.broadcasted_iota(jnp.int32, (E, 1), 0)
    normal = lax.dot_general(
        design, design, (((1,), (1,)), ((), ())), preferred_element_type=jnp.float32
    )
    normal = jnp.where((row == E - 1) & (lane == E - 1), 1.0, normal)
    solved = design
    for i in range(E - 1):
        inverse = 1.0 / normal[i : i + 1, i : i + 1]
        factor = normal[:, i : i + 1]
        factor = jnp.where(rows == i, factor - 1.0, factor)
        lead = normal[i : i + 1, :] * inverse
        other = solved[i : i + 1, :] * inverse
        normal = normal - factor * lead
        solved = solved - factor * other
    below = (lane < row).astype(jnp.float32)
    steps = jnp.dot(below, solved, precision=HIGHEST, preferred_element_type=jnp.float32)
    days = jnp.broadcast_to(days_ref[...].astype(jnp.float32), (E, E))
    times = jnp.sum(jnp.where(row == lane, days, 0.0), axis=1, keepdims=True)
    scaled = (times - jnp.sum(times, axis=0, keepdims=True) / E) / 365.25
    phase = 2.0 * jnp.pi * times / 365.25
    trend = choose(
        lane, [jnp.ones_like(days), scaled, jnp.sin(phase), jnp.cos(phase), jnp.zeros_like(days)]
    )
    turn = (row == lane).astype(jnp.float32)
    for j in range(TREND):
        v = jnp.where(rows >= j, trend[:, j : j + 1], 0.0)
        norm = jnp.sqrt(jnp.sum(v * v, axis=0, keepdims=True))
        head = trend[j : j + 1, j : j + 1]
        v = v + jnp.where(rows == j, jnp.where(head >= 0.0, norm, -norm), 0.0)
        w = v * (2.0 / jnp.sum(v * v, axis=0, keepdims=True))
        trend = trend - w * jnp.sum(v * trend, axis=0, keepdims=True)
        turn = turn - w * jnp.sum(v * turn, axis=0, keepdims=True)
        steps = steps - w * jnp.sum(v * steps, axis=0, keepdims=True)
    shape = (E, E - TREND)
    keep = (
        lax.broadcasted_iota(jnp.int32, shape, 0)
        == lax.broadcasted_iota(jnp.int32, shape, 1) + TREND
    ).astype(jnp.float32)
    basis = jnp.dot(turn.T, keep, precision=HIGHEST, preferred_element_type=jnp.float32)
    narrow = steps[TREND:, :]
    basis_ref[...] = basis
    narrow_ref[...] = narrow
    whole_ref[...] = jnp.dot(basis, narrow, precision=HIGHEST, preferred_element_type=jnp.float32)


def temporal_operator(pair_epochs, days):
    pairs = pair_epochs.shape[1]
    vmem = pl.BlockSpec(memory_space=pltpu.VMEM)
    shapes = [(E, pairs), (E - TREND, pairs), (E, E - TREND)]
    return pl.pallas_call(
        operator_body,
        in_specs=[vmem] * 2,
        out_specs=[vmem] * 3,
        out_shape=[jax.ShapeDtypeStruct(shape, jnp.float32) for shape in shapes],
        compiler_params=pltpu.CompilerParams(vmem_limit_bytes=VMEM_LIMIT),
        name="operator",
    )(pair_epochs, days.reshape(1, E))


def split(x):
    parts = []
    for _ in range(PARTS):
        part = x.astype(jnp.bfloat16)
        parts.append(part)
        x = x - part.astype(jnp.float32)
    return parts


def taps_at(apart):
    far = apart.astype(jnp.float32)
    total = sum(jnp.exp(jnp.float32(-(i * i) / 8.0)) for i in range(-RADIUS, RADIUS + 1))
    return jnp.where(jnp.abs(apart) <= RADIUS, jnp.exp(far * far * -0.125) / total, 0.0)


def choose(index, parts):
    out = parts[0]
    for k in range(1, len(parts)):
        out = jnp.where(index == k, parts[k], out)
    return out


def term_part(index, side):
    out = jnp.zeros_like(index)
    for k, term in enumerate(TERMS):
        out = jnp.where(index == k, term[side], out)
    return out


def smooth_body(mask, make_band, rows, cols, cuts, x_hbm, *refs):
    n_quad = lax.axis_size("quad")
    pair, quad = lax.axis_index("pair"), lax.axis_index("quad")
    local, height, width = x_hbm.shape
    n_out = n_quad * len(cuts)
    if make_band:
        out_refs, band_ref, token_ref = refs[:n_out], refs[n_out], refs[n_out + 1]
    else:
        band_ref, out_refs, token_ref = refs[0], refs[2 : 2 + n_out], refs[2 + n_out]
    xbuf, mid, sems = refs[-3:]
    token_ref[...] = jnp.zeros_like(token_ref)
    reach = xbuf.shape[1]
    high = local * rows
    row0 = lax.bitwise_xor(pair, mask) * rows
    low = pl.multiple_of(jnp.clip(row0 - HALO, 0, height - reach), SUB)
    copies = [
        pltpu.make_async_copy(x_hbm.at[p, pl.ds(low, reach), :], xbuf.at[p], sems.at[p])
        for p in range(local)
    ]
    for copy in copies:
        copy.start()
    if make_band:
        shape = (WIDE + 2 * LANE, WIDE)
        apart = (
            lax.broadcasted_iota(jnp.int32, shape, 1)
            + LANE
            - lax.broadcasted_iota(jnp.int32, shape, 0)
        )
        for k, part in enumerate(split(taps_at(apart))):
            band_ref[k] = part
    shape = (rows, len(TERMS) * reach)
    at = lax.broadcasted_iota(jnp.int32, shape, 1)
    term = at // reach
    apart = lax.broadcasted_iota(jnp.int32, shape, 0) + (row0 - low) - (at - term * reach)
    parts = [part.astype(jnp.float32) for part in split(taps_at(apart))]
    row_band = choose(term_part(term, 0), parts).astype(jnp.bfloat16)
    edge = jnp.zeros((PARTS * high, LANE), jnp.bfloat16)
    mid[:, 0:LANE] = edge
    mid[:, LANE + width : 2 * LANE + width] = edge
    for p in range(local):
        copies[p].wait()
        parts = split(xbuf[p])
        tall = jnp.concatenate([parts[t[1]] for t in TERMS], axis=0)
        done = jnp.dot(row_band, tall, preferred_element_type=jnp.float32)
        for k, part in enumerate(split(done)):
            mid[k * high + p * rows : k * high + (p + 1) * rows, LANE : LANE + width] = part
    for flip in range(n_quad):
        for at in range(0, cols, WIDE):
            start = pl.multiple_of(lax.bitwise_xor(quad, flip) * cols + at, LANE)
            total = None
            for k in reversed(range(PARTS)):
                some = mid[0 : (PARTS - k) * high, pl.ds(start, WIDE + 2 * LANE)]
                done = jnp.dot(some, band_ref[k], preferred_element_type=jnp.float32)
                for j in reversed(range(PARTS - k)):
                    piece = done[j * high : (j + 1) * high]
                    total = piece if total is None else total + piece
            total = total.reshape(local, rows, WIDE)
            top = 0
            for k, size in enumerate(cuts):
                out_ref = out_refs[flip * len(cuts) + k]
                out_ref[:, :, at : at + WIDE] = total[:, top : top + size]
                top += size


def smooth_rows(interferograms, mask, band, token, rows, cols, cuts):
    local, height, width = interferograms.shape
    n_quad = width // cols
    reach = min(height, rows + 2 * HALO)
    vmem = pl.BlockSpec(memory_space=pltpu.VMEM)
    blocks = [jax.ShapeDtypeStruct((local, size, cols), jnp.float32) for size in cuts] * n_quad
    band_shape = jax.ShapeDtypeStruct((PARTS, WIDE + 2 * LANE, WIDE), jnp.bfloat16)
    token_shape = jax.ShapeDtypeStruct((SUB, LANE), jnp.float32)
    make_band = band is None
    where = pl.BlockSpec(memory_space=pltpu.HBM if make_band else pl.ANY)
    if make_band:
        interferograms = pltpu.with_memory_space_constraint(interferograms, pltpu.HBM)
    out = pl.pallas_call(
        functools.partial(smooth_body, mask, make_band, rows, cols, cuts),
        in_specs=[where] + ([] if make_band else [vmem, vmem]),
        out_specs=[vmem] * (len(blocks) + make_band + 1),
        out_shape=blocks + [band_shape] * make_band + [token_shape],
        scratch_shapes=[
            pltpu.VMEM((local, reach, width), jnp.float32),
            pltpu.VMEM((PARTS * local * rows, width + 2 * LANE), jnp.bfloat16),
            pltpu.SemaphoreType.DMA((local,)),
        ],
        cost_estimate=pl.CostEstimate(
            flops=2 * local * rows * width * 6 * 768,
            bytes_accessed=4 * local * (rows + reach) * width,
            transcendentals=0,
        ),
        compiler_params=pltpu.CompilerParams(vmem_limit_bytes=VMEM_LIMIT),
    )(interferograms, *([] if make_band else [band, token]))
    n_cuts = len(cuts)
    blocks = [out[flip * n_cuts : (flip + 1) * n_cuts] for flip in range(n_quad)]
    return blocks, (out[len(blocks) * n_cuts] if make_band else band), out[-1]


def expand_body(masks, local, op_ref, out_ref):
    n_quad = lax.axis_size("quad")
    me = lax.axis_index("pair") * n_quad + lax.axis_index("quad")
    tall, broad = out_ref.shape
    lines, pairs = op_ref.shape
    depth = broad // len(TERMS)
    shape = (tall, lines)
    repeat = (
        lax.broadcasted_iota(jnp.int32, shape, 0) // SUB
        == lax.broadcasted_iota(jnp.int32, shape, 1)
    ).astype(jnp.float32)
    shape = (pairs, broad)
    at = lax.broadcasted_iota(jnp.int32, shape, 1) % depth
    source = at // SUB
    if masks is not None:
        block = source // local
        mask = jnp.zeros_like(block)
        for k, value in enumerate(masks):
            mask = jnp.where(block == k, value, mask)
        source = lax.bitwise_xor(me, mask) * local + source % local
    place = (source == lax.broadcasted_iota(jnp.int32, shape, 0)).astype(jnp.float32)
    both = jnp.dot(repeat, op_ref[...], precision=HIGHEST, preferred_element_type=jnp.float32)
    both = jnp.dot(both, place, precision=HIGHEST, preferred_element_type=jnp.float32)
    shape = (tall, broad)
    at = lax.broadcasted_iota(jnp.int32, shape, 1)
    same = at % SUB == lax.broadcasted_iota(jnp.int32, shape, 0) % SUB
    parts = [part.astype(jnp.float32) for part in split(jnp.where(same, both, 0.0))]
    out_ref[...] = choose(term_part(at // depth, 0), parts).astype(jnp.bfloat16)


def expand(operator, masks, local):
    lines, pairs = operator.shape
    depth = (pairs if masks is None else len(masks) * local) * SUB
    return pl.pallas_call(
        functools.partial(expand_body, masks, local),
        in_specs=[pl.BlockSpec(memory_space=pltpu.VMEM)],
        out_specs=pl.BlockSpec(memory_space=pltpu.VMEM),
        out_shape=jax.ShapeDtypeStruct((lines * SUB, len(TERMS) * depth), jnp.bfloat16),
        compiler_params=pltpu.CompilerParams(vmem_limit_bytes=VMEM_LIMIT),
    )(operator)


def product(weights, stacks, at):
    span = pl.ds(at, SUB)
    x = jnp.concatenate([ref[:, span, :].reshape(-1, ref.shape[2]) for ref in stacks], axis=0)
    parts = split(x)
    tall = jnp.concatenate([parts[t[1]] for t in TERMS], axis=0)
    total = jnp.dot(weights, tall, preferred_element_type=jnp.float32)
    return total.reshape(-1, SUB, total.shape[1])


def apply_body(n_in, starts, has_acc, w_ref, *refs):
    x_refs, out_ref = refs[:n_in], refs[-1]
    for k, at in enumerate(starts):
        total = product(w_ref[...], x_refs, at)
        if has_acc:
            total = total + refs[n_in][:, pl.ds(k * SUB, SUB), :]
        out_ref[:, pl.ds(k * SUB, SUB), :] = total


def apply_operator(weights, stacks, acc, starts):
    cols = stacks[0].shape[2]
    lines = weights.shape[0] // SUB
    vmem = pl.BlockSpec(memory_space=pltpu.VMEM)
    extra = [] if acc is None else [acc]
    count = len(starts) * SUB
    return pl.pallas_call(
        functools.partial(apply_body, len(stacks), starts, acc is not None),
        in_specs=[vmem] * (1 + len(stacks) + len(extra)),
        out_specs=vmem,
        out_shape=jax.ShapeDtypeStruct((lines, count, cols), jnp.float32),
        cost_estimate=pl.CostEstimate(
            flops=2 * weights.shape[0] * weights.shape[1] * len(starts) * cols,
            bytes_accessed=4 * count * cols * (len(stacks) * stacks[0].shape[0] + lines),
            transcendentals=0,
        ),
        compiler_params=pltpu.CompilerParams(vmem_limit_bytes=VMEM_LIMIT),
    )(weights, *stacks, *extra)


def finish_body(n_in, starts, top, skip, has_out, w_ref, *refs):
    x_refs, acc_ref = refs[:n_in], refs[n_in]
    out_hbm, buf, sems = refs[n_in + 1 + has_out :]
    copies = []
    for k, at in enumerate(starts):
        buf[k] = product(w_ref[...], x_refs, at) + acc_ref[:, pl.ds(skip + k * SUB, SUB), :]
        rows = pl.ds(top + k * SUB, SUB)
        copies.append(pltpu.make_async_copy(buf.at[k], out_hbm.at[:, rows, :], sems.at[k]))
        copies[-1].start()
    for copy in copies:
        copy.wait()


def finish(weights, stacks, acc, starts, top, skip, out, rows):
    cols = stacks[0].shape[2]
    n_in, count = len(stacks), len(starts)
    vmem = pl.BlockSpec(memory_space=pltpu.VMEM)
    hbm = pl.BlockSpec(memory_space=pltpu.HBM)
    extra = [] if out is None else [out]
    return pl.pallas_call(
        functools.partial(finish_body, n_in, starts, top, skip, len(extra)),
        in_specs=[vmem] * (n_in + 2) + [hbm] * len(extra),
        out_specs=hbm,
        out_shape=jax.ShapeDtypeStruct((E, rows, cols), jnp.float32),
        input_output_aliases={n_in + 2: 0} if extra else {},
        scratch_shapes=[
            pltpu.VMEM((count, E, SUB, cols), jnp.float32),
            pltpu.SemaphoreType.DMA((count,)),
        ],
        cost_estimate=pl.CostEstimate(
            flops=2 * weights.shape[0] * weights.shape[1] * count * cols,
            bytes_accessed=4 * count * SUB * cols * (n_in * stacks[0].shape[0] + 2 * E),
            transcendentals=0,
        ),
        compiler_params=pltpu.CompilerParams(vmem_limit_bytes=VMEM_LIMIT),
    )(weights, *stacks, acc, *extra)


class Plan:
    def __init__(self, n_pair, n_quad, rows):
        self.devices = n_pair * n_quad
        self.half = self.devices // 2
        far = list(range(n_pair // 2, n_pair))
        middle = len(far) // 2
        self.far = far[middle:] + far[:middle]
        near = list(range(n_pair // 4, n_pair // 2))
        self.near = near
        self.rest = list(range(n_pair // 4))[::-1]
        groups = rows // SUB
        self.merged = list(range(groups - max(1, groups // 2), groups))
        self.plain = list(range(self.merged[0]))
        self.split = self.merged[0] * SUB


def shards(interferograms, pair_epochs, days):
    n_pair = lax.axis_size("pair")
    n_quad = lax.axis_size("quad")
    local, height, width = interferograms.shape
    rows = height // n_pair
    cols = width // n_quad
    plan = Plan(n_pair, n_quad, rows)
    half = plan.half
    state = [None, None]

    def smooth(mask, cuts):
        blocks, state[0], state[1] = smooth_rows(
            interferograms, mask, *state, rows, cols, cuts
        )
        return blocks

    def send(block, which):
        if which == 0:
            return block
        route = [(i, i ^ which) for i in range(plan.devices)]
        return lax.ppermute(block, AXES, route)

    plain, gathered, own = {}, {}, {}
    for mask in plan.far:
        blocks = smooth(mask, (plan.split, rows - plan.split))
        for flip, (first, second) in enumerate(blocks):
            which = mask * n_quad + flip
            gathered[which - half] = send(second, which - half)
            plain[which] = send(first, which)
    whole, narrow, basis = temporal_operator(pair_epochs, days)
    everyone = list(range(half))
    weights = expand(narrow, everyone, local)
    arrived = []
    for k in range(len(plan.merged)):
        some = apply_operator(weights, [gathered[w] for w in everyone], None, [k * SUB])
        arrived.append(send(some, half))
    for mask in plan.near + plan.rest:
        for flip, (block,) in enumerate(smooth(mask, (rows,))):
            which = mask * n_quad + flip
            own[which] = send(block, which)
    total = None
    starts = [k * SUB for k in plan.plain]
    left = [mask * n_quad + flip for mask in plan.far for flip in range(n_quad)]
    weights = expand(whole, left, local)
    total = apply_operator(weights, [plain[w] for w in left], None, starts)
    weights = expand(whole, everyone, local)
    stacks = [own[w] for w in everyone]
    out = finish(weights, stacks, total, starts, 0, 0, None, rows)
    later = [k * SUB for k in plan.merged]
    total = apply_operator(weights, stacks, None, later)
    weights = expand(basis, None, local)
    for k, group in enumerate(plan.merged):
        top = group * SUB
        out = finish(weights, [arrived[k]], total, [0], top, k * SUB, out, rows)
    return out


def solution(mesh):
    placed = (P(("pair", "quad"), "slab", None), P(), P())

    def step(interferograms, pair_epochs, days):
        mapped = jax.shard_map(
            shards,
            mesh=mesh,
            in_specs=placed,
            out_specs=P(None, ("slab", "pair"), "quad"),
            check_vma=False,
        )
        return mapped(interferograms, pair_epochs, days)

    return step
```

profile of v0, /device:TPU:0, one launch (start us, length us, event | category | flops | bytes accessed | tf_op | source)
XLA Modules:
  0.0 129.5 jit_solution(1639111441052563206)
XLA Ops:
  0.0 3.0 %shard_map.39 = (f32[4,16,512]{2,1,0:T(8,128)S(1)}, f32[4,16,512]{2,1,0:T(8,128)S(1)}, f32[4,16,512]{2,1,0:T(8,128)S(1)}, f32[4,16,512]{2,1,0:T(8,128)S(1)}, bf1...) custom-call(f32[4,256,1024]{2,1,0:T(8,128)} %x_hbm.15), custom_call_target="tpu_custom_call" | custom-call | flops 1207959552 | bytes 1310720 | tf_op jit(solution)/shard_map/pallas_call | solution.py:196
  3.0 3.0 %shard_map.40 = (f32[4,16,512]{2,1,0:T(8,128)S(1)}, f32[4,16,512]{2,1,0:T(8,128)S(1)}, f32[4,16,512]{2,1,0:T(8,128)S(1)}, f32[4,16,512]{2,1,0:T(8,128)S(1)}, f32[8,128]{1,0:T(8,128)S(1)}) custom-call(f32[4,256,1024]{2,1,0:T(8,128)S(1)} %copy-done, bf16[3,512,256]{2,1,0:T(8,128)(2,1)S(1)} %get-tuple-element.42.refs_0_, f32[8,128]{1,0:T(8,128)S(1)} %get-tuple-element.43.refs_1_), custom_call_target="tpu_custom_call" | custom-call | flops 1207959552 | bytes 1310720 | tf_op jit(solution)/shard_map/pallas_call | solution.py:196
  6.1 3.0 %shard_map.41 = (f32[4,16,512]{2,1,0:T(8,128)S(1)}, f32[4,16,512]{2,1,0:T(8,128)S(1)}, f32[4,16,512]{2,1,0:T(8,128)S(1)}, f32[4,16,512]{2,1,0:T(8,128)S(1)}, f32[8,128]{1,0:T(8,128)S(1)}) custom-call(f32[4,256,1024]{2,1,0:T(8,128)S(1)} %copy-done, bf16[3,512,256]{2,1,0:T(8,128)(2,1)S(1)} %get-tuple-element.42.refs_0_, f32[8,128]{1,0:T(8,128)S(1)} %get-tuple-element.44.refs_1_), custom_call_target="tpu_custom_call" | custom-call | flops 1207959552 | bytes 1310720 | tf_op jit(solution)/shard_map/pallas_call | solution.py:196
  9.1 3.0 %shard_map.42 = (f32[4,16,512]{2,1,0:T(8,128)S(1)}, f32[4,16,512]{2,1,0:T(8,128)S(1)}, f32[4,16,512]{2,1,0:T(8,128)S(1)}, f32[4,16,512]{2,1,0:T(8,128)S(1)}, f32[8,128]{1,0:T(8,128)S(1)}) custom-call(f32[4,256,1024]{2,1,0:T(8,128)S(1)} %copy-done, bf16[3,512,256]{2,1,0:T(8,128)(2,1)S(1)} %get-tuple-element.42.refs_0_, f32[8,128]{1,0:T(8,128)S(1)} %get-tuple-element.47.refs_1_), custom_call_target="tpu_custom_call" | custom-call | flops 1207959552 | bytes 1310720 | tf_op jit(solution)/shard_map/pallas_call | solution.py:196
  12.1 5.1 %collective-permute-start.22 = (f32[4,16,512]{2,1,0:T(8,128)S(1)}, f32[4,16,512]{2,1,0:T(8,128)S(1)}, u32[]{:S(2)}, u32[]{:S(2)}) collective-permute-start(f32[4,16,512]{2,1,0:T(8,128)S(1)} %get-tuple-element.73), channel_id=1, source_target_pairs={{0,10},{1,11},{2,8},{3,9},{4,14},{5,15},{6,12},{7,13},{8,2},{9,3},... | collective-permute-start | bytes 393224 | tf_op jit(solution)/shard_map/ppermute | solution.py:372
  17.2 2.0 %collective-permute-start.20 = (f32[4,16,512]{2,1,0:T(8,128)S(1)}, f32[4,16,512]{2,1,0:T(8,128)S(1)}, u32[]{:S(2)}, u32[]{:S(2)}) collective-permute-start(f32[4,16,512]{2,1,0:T(8,128)S(1)} %get-tuple-element.71), channel_id=1, source_target_pairs={{0,8},{1,9},{2,10},{3,11},{4,12},{5,13},{6,14},{7,15},{8,0},{9,1},... | collective-permute-start | bytes 393224 | tf_op jit(solution)/shard_map/ppermute | solution.py:372
  19.8 4.6 %collective-permute-start.18 = (f32[4,16,512]{2,1,0:T(8,128)S(1)}, f32[4,16,512]{2,1,0:T(8,128)S(1)}, u32[]{:S(2)}, u32[]{:S(2)}) collective-permute-start(f32[4,16,512]{2,1,0:T(8,128)S(1)} %get-tuple-element.69), channel_id=1, source_target_pairs={{0,14},{1,15},{2,12},{3,13},{4,10},{5,11},{6,8},{7,9},{8,6},{9,7},... | collective-permute-start | bytes 393224 | tf_op jit(solution)/shard_map/ppermute | solution.py:372
  24.4 11.2 %collective-permute-done.22.refs_6_ = f32[4,16,512]{2,1,0:T(8,128)S(1)} collective-permute-done((f32[4,16,512]{2,1,0:T(8,128)S(1)}, f32[4,16,512]{2,1,0:T(8,128)S(1)}, u32[]{:S(2)}, u32[]{:S(2)}) %collective-permute-start.22) | collective-permute-done | bytes 131104 | tf_op jit(solution)/shard_map/ppermute | solution.py:372
  35.6 3.2 %collective-permute-start.19 = (f32[4,16,512]{2,1,0:T(8,128)S(1)}, f32[4,16,512]{2,1,0:T(8,128)S(1)}, u32[]{:S(2)}, u32[]{:S(2)}) collective-permute-start(f32[4,16,512]{2,1,0:T(8,128)S(1)} %get-tuple-element.70), channel_id=1, source_target_pairs={{0,15},{1,14},{2,13},{3,12},{4,11},{5,10},{6,9},{7,8},{8,7},{9,6},... | collective-permute-start | bytes 393224 | tf_op jit(solution)/shard_map/ppermute | solution.py:372
  38.8 2.1 %collective-permute-start.16 = (f32[4,16,512]{2,1,0:T(8,128)S(1)}, f32[4,16,512]{2,1,0:T(8,128)S(1)}, u32[]{:S(2)}, u32[]{:S(2)}) collective-permute-start(f32[4,16,512]{2,1,0:T(8,128)S(1)} %get-tuple-element.67), channel_id=1, source_target_pairs={{0,12},{1,13},{2,14},{3,15},{4,8},{5,9},{6,10},{7,11},{8,4},{9,5},... | collective-permute-start | bytes 393224 | tf_op jit(solution)/shard_map/ppermute | solution.py:372
  40.9 6.2 %collective-permute-done.20.refs_4_ = f32[4,16,512]{2,1,0:T(8,128)S(1)} collective-permute-done((f32[4,16,512]{2,1,0:T(8,128)S(1)}, f32[4,16,512]{2,1,0:T(8,128)S(1)}, u32[]{:S(2)}, u32[]{:S(2)}) %collective-permute-start.20) | collective-permute-done | bytes 131104 | tf_op jit(solution)/shard_map/ppermute | solution.py:372
  47.4 3.0 %shard_map.45 = (f32[4,32,512]{2,1,0:T(8,128)S(1)}, f32[4,32,512]{2,1,0:T(8,128)S(1)}, f32[8,128]{1,0:T(8,128)S(1)}) custom-call(f32[4,256,1024]{2,1,0:T(8,128)S(1)} %copy-done, bf16[3,512,256]{2,1,0:T(8,128)(2,1)S(1)} %get-tuple-element.42.refs_0_, f32[8,128]{1,0:T(8,128)S(1)} %get-tuple-element.55.refs_1_), custom_call_target="tpu_custom_call" | custom-call | flops 1207959552 | bytes 1310720 | tf_op jit(solution)/shard_map/pallas_call | solution.py:196
  50.4 3.0 %shard_map.46 = (f32[4,32,512]{2,1,0:T(8,128)S(1)}, f32[4,32,512]{2,1,0:T(8,128)S(1)}, f32[8,128]{1,0:T(8,128)S(1)}) custom-call(f32[4,256,1024]{2,1,0:T(8,128)S(1)} %copy-done, bf16[3,512,256]{2,1,0:T(8,128)(2,1)S(1)} %get-tuple-element.42.refs_0_, f32[8,128]{1,0:T(8,128)S(1)} %get-tuple-element.56.refs_1_), custom_call_target="tpu_custom_call" | custom-call | flops 1207959552 | bytes 1310720 | tf_op jit(solution)/shard_map/pallas_call | solution.py:196
  55.3 2.3 %collective-permute-start.6 = (f32[4,16,512]{2,1,0:T(8,128)S(1)}, f32[4,16,512]{2,1,0:T(8,128)S(1)}, u32[]{:S(2)}, u32[]{:S(2)}) collective-permute-start(f32[4,16,512]{2,1,0:T(8,128)S(1)} %get-tuple-element.53), channel_id=1, source_target_pairs={{0,7},{1,6},{2,5},{3,4},{4,3},{5,2},{6,1},{7,0},{8,15},{9,14},{10,... | collective-permute-start | bytes 393224 | tf_op jit(solution)/shard_map/ppermute | solution.py:372
  57.9 3.0 %shard_map.47 = (f32[4,32,512]{2,1,0:T(8,128)S(1)}, f32[4,32,512]{2,1,0:T(8,128)S(1)}, f32[8,128]{1,0:T(8,128)S(1)}) custom-call(f32[4,256,1024]{2,1,0:T(8,128)S(1)} %copy-done, bf16[3,512,256]{2,1,0:T(8,128)(2,1)S(1)} %get-tuple-element.42.refs_0_, f32[8,128]{1,0:T(8,128)S(1)} %get-tuple-element.57.refs_1_), custom_call_target="tpu_custom_call" | custom-call | flops 1207959552 | bytes 1310720 | tf_op jit(solution)/shard_map/pallas_call | solution.py:196
  62.8 3.4 %shard_map.48 = (f32[4,32,512]{2,1,0:T(8,128)S(1)}, f32[4,32,512]{2,1,0:T(8,128)S(1)}, f32[8,128]{1,0:T(8,128)}) custom-call(f32[4,256,1024]{2,1,0:T(8,128)S(1)} %copy-done, bf16[3,512,256]{2,1,0:T(8,128)(2,1)S(1)} %get-tuple-element.42.refs_0_, f32[8,128]{1,0:T(8,128)S(1)} %get-tuple-element.58.refs_1_), custom_call_target="tpu_custom_call" | custom-call | flops 1207959552 | bytes 1310720 | tf_op jit(solution)/shard_map/pallas_call | solution.py:196
  69.5 2.4 %collective-permute-start.17 = (f32[4,16,512]{2,1,0:T(8,128)S(1)}, f32[4,16,512]{2,1,0:T(8,128)S(1)}, u32[]{:S(2)}, u32[]{:S(2)}) collective-permute-start(f32[4,16,512]{2,1,0:T(8,128)S(1)} %get-tuple-element.68), channel_id=1, source_target_pairs={{0,13},{1,12},{2,15},{3,14},{4,9},{5,8},{6,11},{7,10},{8,5},{9,4},... | collective-permute-start | bytes 393224 | tf_op jit(solution)/shard_map/ppermute | solution.py:372
  71.9 3.1 %operator.1 = (f32[32,64]{1,0:T(8,128)S(1)}, f32[28,64]{1,0:T(8,128)S(1)}, f32[32,28]{1,0:T(8,128)S(1)}) custom-call(s32[2,64]{1,0:T(2,128)S(1)} %copy-done.1, s32[1,32]{1,0:T(1,128)S(1)} %bitcast.1), custom_call_target="tpu_custom_call" | custom-call | tf_op jit(solution)/shard_map/operator/pallas_call | solution.py:81
  77.1 3.4 %collective-permute-done.17.refs_1_ = f32[4,16,512]{2,1,0:T(8,128)S(1)} collective-permute-done((f32[4,16,512]{2,1,0:T(8,128)S(1)}, f32[4,16,512]{2,1,0:T(8,128)S(1)}, u32[]{:S(2)}, u32[]{:S(2)}) %collective-permute-start.17) | collective-permute-done | bytes 131104 | tf_op jit(solution)/shard_map/ppermute | solution.py:372
  81.1 3.0 %collective-permute-start.7 = (f32[28,8,512]{2,1,0:T(8,128)S(1)}, f32[28,8,512]{2,1,0:T(8,128)S(1)}, u32[]{:S(2)}, u32[]{:S(2)}) collective-permute-start(f32[28,8,512]{2,1,0:T(8,128)S(1)} %shard_map.43), channel_id=1, source_target_pairs={{0,8},{1,9},{2,10},{3,11},{4,12},{5,13},{6,14},{7,15},{8,0},{9,1},... | collective-permute-start | bytes 1376264 | tf_op jit(solution)/shard_map/ppermute | solution.py:372
  84.1 2.1 %collective-permute-done.9.refs_2_ = f32[4,32,512]{2,1,0:T(8,128)S(1)} collective-permute-done((f32[4,32,512]{2,1,0:T(8,128)S(1)}, f32[4,32,512]{2,1,0:T(8,128)S(1)}, u32[]{:S(2)}, u32[]{:S(2)}) %collective-permute-start.9) | collective-permute-done | bytes 262176 | tf_op jit(solution)/shard_map/ppermute | solution.py:372
  93.3 13.5 %collective-permute-done.14.refs_7_ = f32[4,32,512]{2,1,0:T(8,128)S(1)} collective-permute-done((f32[4,32,512]{2,1,0:T(8,128)S(1)}, f32[4,32,512]{2,1,0:T(8,128)S(1)}, u32[]{:S(2)}, u32[]{:S(2)}) %collective-permute-start.14) | collective-permute-done | bytes 262176 | tf_op jit(solution)/shard_map/ppermute | solution.py:372
  106.8 5.6 %collective-permute-done.11.refs_4_ = f32[4,32,512]{2,1,0:T(8,128)S(1)} collective-permute-done((f32[4,32,512]{2,1,0:T(8,128)S(1)}, f32[4,32,512]{2,1,0:T(8,128)S(1)}, u32[]{:S(2)}, u32[]{:S(2)}) %collective-permute-start.11) | collective-permute-done | bytes 262176 | tf_op jit(solution)/shard_map/ppermute | solution.py:372
  112.4 11.3 %collective-permute-done.12.refs_5_ = f32[4,32,512]{2,1,0:T(8,128)S(1)} collective-permute-done((f32[4,32,512]{2,1,0:T(8,128)S(1)}, f32[4,32,512]{2,1,0:T(8,128)S(1)}, u32[]{:S(2)}, u32[]{:S(2)}) %collective-permute-start.12) | collective-permute-done | bytes 262176 | tf_op jit(solution)/shard_map/ppermute | solution.py:372
  (50 shorter events, 23.6 us)
Async XLA Ops:
  12.1 23.5 %collective-permute-start.22 = (f32[4,16,512]{2,1,0:T(8,128)S(1)}, f32[4,16,512]{2,1,0:T(8,128)S(1)}, u32[]{:S(2)}, u32[]{:S(2)}) collective-permute-start(f32[4,16,512]{2,1,0:T(8,128)S(1)} %get-tuple-element.73), channel_id=1, source_target_pairs={{0,10},{1,11},{2,8},{3,9},{4,14},{5,15},{6,12},{7,13},{8,2},{9,3},... | collective-permute-start | bytes 393224 | tf_op jit(solution)/shard_map/ppermute | solution.py:372
  17.2 21.6 %collective-permute-start.23 = (f32[4,16,512]{2,1,0:T(8,128)S(1)}, f32[4,16,512]{2,1,0:T(8,128)S(1)}, u32[]{:S(2)}, u32[]{:S(2)}) collective-permute-start(f32[4,16,512]{2,1,0:T(8,128)S(1)} %get-tuple-element.74), channel_id=1, source_target_pairs={{0,11},{1,10},{2,9},{3,8},{4,15},{5,14},{6,13},{7,12},{8,3},{9,2},... | collective-permute-start | bytes 393224 | tf_op jit(solution)/shard_map/ppermute | solution.py:372
  17.2 29.9 %collective-permute-start.20 = (f32[4,16,512]{2,1,0:T(8,128)S(1)}, f32[4,16,512]{2,1,0:T(8,128)S(1)}, u32[]{:S(2)}, u32[]{:S(2)}) collective-permute-start(f32[4,16,512]{2,1,0:T(8,128)S(1)} %get-tuple-element.71), channel_id=1, source_target_pairs={{0,8},{1,9},{2,10},{3,11},{4,12},{5,13},{6,14},{7,15},{8,0},{9,1},... | collective-permute-start | bytes 393224 | tf_op jit(solution)/shard_map/ppermute | solution.py:372
  19.2 31.1 %collective-permute-start.21 = (f32[4,16,512]{2,1,0:T(8,128)S(1)}, f32[4,16,512]{2,1,0:T(8,128)S(1)}, u32[]{:S(2)}, u32[]{:S(2)}) collective-permute-start(f32[4,16,512]{2,1,0:T(8,128)S(1)} %get-tuple-element.72), channel_id=1, source_target_pairs={{0,9},{1,8},{2,11},{3,10},{4,13},{5,12},{6,15},{7,14},{8,1},{9,0},... | collective-permute-start | bytes 393224 | tf_op jit(solution)/shard_map/ppermute | solution.py:372
  19.8 33.7 %collective-permute-start.18 = (f32[4,16,512]{2,1,0:T(8,128)S(1)}, f32[4,16,512]{2,1,0:T(8,128)S(1)}, u32[]{:S(2)}, u32[]{:S(2)}) collective-permute-start(f32[4,16,512]{2,1,0:T(8,128)S(1)} %get-tuple-element.69), channel_id=1, source_target_pairs={{0,14},{1,15},{2,12},{3,13},{4,10},{5,11},{6,8},{7,9},{8,6},{9,7},... | collective-permute-start | bytes 393224 | tf_op jit(solution)/shard_map/ppermute | solution.py:372
  35.6 19.8 %collective-permute-start.19 = (f32[4,16,512]{2,1,0:T(8,128)S(1)}, f32[4,16,512]{2,1,0:T(8,128)S(1)}, u32[]{:S(2)}, u32[]{:S(2)}) collective-permute-start(f32[4,16,512]{2,1,0:T(8,128)S(1)} %get-tuple-element.70), channel_id=1, source_target_pairs={{0,15},{1,14},{2,13},{3,12},{4,11},{5,10},{6,9},{7,8},{8,7},{9,6},... | collective-permute-start | bytes 393224 | tf_op jit(solution)/shard_map/ppermute | solution.py:372
  38.8 16.6 %collective-permute-start.16 = (f32[4,16,512]{2,1,0:T(8,128)S(1)}, f32[4,16,512]{2,1,0:T(8,128)S(1)}, u32[]{:S(2)}, u32[]{:S(2)}) collective-permute-start(f32[4,16,512]{2,1,0:T(8,128)S(1)} %get-tuple-element.67), channel_id=1, source_target_pairs={{0,12},{1,13},{2,14},{3,15},{4,8},{5,9},{6,10},{7,11},{8,4},{9,5},... | collective-permute-start | bytes 393224 | tf_op jit(solution)/shard_map/ppermute | solution.py:372
  47.1 10.6 %collective-permute-start.1 = (f32[4,16,512]{2,1,0:T(8,128)S(1)}, f32[4,16,512]{2,1,0:T(8,128)S(1)}, u32[]{:S(2)}, u32[]{:S(2)}) collective-permute-start(f32[4,16,512]{2,1,0:T(8,128)S(1)} %get-tuple-element.48), channel_id=1, source_target_pairs={{0,2},{1,3},{2,0},{3,1},{4,6},{5,7},{6,4},{7,5},{8,10},{9,11},{10,... | collective-permute-start | bytes 393224 | tf_op jit(solution)/shard_map/ppermute | solution.py:372
  50.3 10.6 %collective-permute-start.2 = (f32[4,16,512]{2,1,0:T(8,128)S(1)}, f32[4,16,512]{2,1,0:T(8,128)S(1)}, u32[]{:S(2)}, u32[]{:S(2)}) collective-permute-start(f32[4,16,512]{2,1,0:T(8,128)S(1)} %get-tuple-element.49), channel_id=1, source_target_pairs={{0,3},{1,2},{2,1},{3,0},{4,7},{5,6},{6,5},{7,4},{8,11},{9,10},{10,... | collective-permute-start | bytes 393224 | tf_op jit(solution)/shard_map/ppermute | solution.py:372
  53.4 12.8 %collective-permute-start = (f32[4,16,512]{2,1,0:T(8,128)S(1)}, f32[4,16,512]{2,1,0:T(8,128)S(1)}, u32[]{:S(2)}, u32[]{:S(2)}) collective-permute-start(f32[4,16,512]{2,1,0:T(8,128)S(1)} %get-tuple-element.46), channel_id=1, source_target_pairs={{0,1},{1,0},{2,3},{3,2},{4,5},{5,4},{6,7},{7,6},{8,9},{9,8},{10,11... | collective-permute-start | bytes 393224 | tf_op jit(solution)/shard_map/ppermute | solution.py:372
  55.3 11.0 %collective-permute-start.5 = (f32[4,16,512]{2,1,0:T(8,128)S(1)}, f32[4,16,512]{2,1,0:T(8,128)S(1)}, u32[]{:S(2)}, u32[]{:S(2)}) collective-permute-start(f32[4,16,512]{2,1,0:T(8,128)S(1)} %get-tuple-element.52), channel_id=1, source_target_pairs={{0,6},{1,7},{2,4},{3,5},{4,2},{5,3},{6,0},{7,1},{8,14},{9,15},{10,... | collective-permute-start | bytes 393224 | tf_op jit(solution)/shard_map/ppermute | solution.py:372
  55.3 12.2 %collective-permute-start.6 = (f32[4,16,512]{2,1,0:T(8,128)S(1)}, f32[4,16,512]{2,1,0:T(8,128)S(1)}, u32[]{:S(2)}, u32[]{:S(2)}) collective-permute-start(f32[4,16,512]{2,1,0:T(8,128)S(1)} %get-tuple-element.53), channel_id=1, source_target_pairs={{0,7},{1,6},{2,5},{3,4},{4,3},{5,2},{6,1},{7,0},{8,15},{9,14},{10,... | collective-permute-start | bytes 393224 | tf_op jit(solution)/shard_map/ppermute | solution.py:372
  57.7 10.8 %collective-permute-start.3 = (f32[4,16,512]{2,1,0:T(8,128)S(1)}, f32[4,16,512]{2,1,0:T(8,128)S(1)}, u32[]{:S(2)}, u32[]{:S(2)}) collective-permute-start(f32[4,16,512]{2,1,0:T(8,128)S(1)} %get-tuple-element.50), channel_id=1, source_target_pairs={{0,4},{1,5},{2,6},{3,7},{4,0},{5,1},{6,2},{7,3},{8,12},{9,13},{10,... | collective-permute-start | bytes 393224 | tf_op jit(solution)/shard_map/ppermute | solution.py:372
  60.9 8.6 %collective-permute-start.4 = (f32[4,16,512]{2,1,0:T(8,128)S(1)}, f32[4,16,512]{2,1,0:T(8,128)S(1)}, u32[]{:S(2)}, u32[]{:S(2)}) collective-permute-start(f32[4,16,512]{2,1,0:T(8,128)S(1)} %get-tuple-element.51), channel_id=1, source_target_pairs={{0,5},{1,4},{2,7},{3,6},{4,1},{5,0},{6,3},{7,2},{8,13},{9,12},{10,... | collective-permute-start | bytes 393224 | tf_op jit(solution)/shard_map/ppermute | solution.py:372
  66.2 14.9 %collective-permute-start.8 = (f32[4,32,512]{2,1,0:T(8,128)S(1)}, f32[4,32,512]{2,1,0:T(8,128)S(1)}, u32[]{:S(2)}, u32[]{:S(2)}) collective-permute-start(f32[4,32,512]{2,1,0:T(8,128)S(1)} %get-tuple-element.60), channel_id=1, source_target_pairs={{0,1},{1,0},{2,3},{3,2},{4,5},{5,4},{6,7},{7,6},{8,9},{9,8},{10,11... | collective-permute-start | bytes 786440 | tf_op jit(solution)/shard_map/ppermute | solution.py:372
  66.4 17.7 %collective-permute-start.10 = (f32[4,32,512]{2,1,0:T(8,128)S(1)}, f32[4,32,512]{2,1,0:T(8,128)S(1)}, u32[]{:S(2)}, u32[]{:S(2)}) collective-permute-start(f32[4,32,512]{2,1,0:T(8,128)S(1)} %get-tuple-element.62), channel_id=1, source_target_pairs={{0,3},{1,2},{2,1},{3,0},{4,7},{5,6},{6,5},{7,4},{8,11},{9,10},{10,... | collective-permute-start | bytes 786440 | tf_op jit(solution)/shard_map/ppermute | solution.py:372
  67.6 18.7 %collective-permute-start.9 = (f32[4,32,512]{2,1,0:T(8,128)S(1)}, f32[4,32,512]{2,1,0:T(8,128)S(1)}, u32[]{:S(2)}, u32[]{:S(2)}) collective-permute-start(f32[4,32,512]{2,1,0:T(8,128)S(1)} %get-tuple-element.61), channel_id=1, source_target_pairs={{0,2},{1,3},{2,0},{3,1},{4,6},{5,7},{6,4},{7,5},{8,10},{9,11},{10,... | collective-permute-start | bytes 786440 | tf_op jit(solution)/shard_map/ppermute | solution.py:372
  68.4 18.1 %collective-permute-start.13 = (f32[4,32,512]{2,1,0:T(8,128)S(1)}, f32[4,32,512]{2,1,0:T(8,128)S(1)}, u32[]{:S(2)}, u32[]{:S(2)}) collective-permute-start(f32[4,32,512]{2,1,0:T(8,128)S(1)} %get-tuple-element.65), channel_id=1, source_target_pairs={{0,6},{1,7},{2,4},{3,5},{4,2},{5,3},{6,0},{7,1},{8,14},{9,15},{10,... | collective-permute-start | bytes 786440 | tf_op jit(solution)/shard_map/ppermute | solution.py:372
  69.5 11.0 %collective-permute-start.17 = (f32[4,16,512]{2,1,0:T(8,128)S(1)}, f32[4,16,512]{2,1,0:T(8,128)S(1)}, u32[]{:S(2)}, u32[]{:S(2)}) collective-permute-start(f32[4,16,512]{2,1,0:T(8,128)S(1)} %get-tuple-element.68), channel_id=1, source_target_pairs={{0,13},{1,12},{2,15},{3,14},{4,9},{5,8},{6,11},{7,10},{8,5},{9,4},... | collective-permute-start | bytes 393224 | tf_op jit(solution)/shard_map/ppermute | solution.py:372
  80.6 46.0 %collective-permute-start.15 = (f32[28,8,512]{2,1,0:T(8,128)S(1)}, f32[28,8,512]{2,1,0:T(8,128)S(1)}, u32[]{:S(2)}, u32[]{:S(2)}) collective-permute-start(f32[28,8,512]{2,1,0:T(8,128)S(1)} %shard_map.50), channel_id=1, source_target_pairs={{0,8},{1,9},{2,10},{3,11},{4,12},{5,13},{6,14},{7,15},{8,0},{9,1},... | collective-permute-start | bytes 1376264 | tf_op jit(solution)/shard_map/ppermute | solution.py:372
  81.1 46.8 %collective-permute-start.7 = (f32[28,8,512]{2,1,0:T(8,128)S(1)}, f32[28,8,512]{2,1,0:T(8,128)S(1)}, u32[]{:S(2)}, u32[]{:S(2)}) collective-permute-start(f32[28,8,512]{2,1,0:T(8,128)S(1)} %shard_map.43), channel_id=1, source_target_pairs={{0,8},{1,9},{2,10},{3,11},{4,12},{5,13},{6,14},{7,15},{8,0},{9,1},... | collective-permute-start | bytes 1376264 | tf_op jit(solution)/shard_map/ppermute | solution.py:372
  84.1 22.7 %collective-permute-start.14 = (f32[4,32,512]{2,1,0:T(8,128)S(1)}, f32[4,32,512]{2,1,0:T(8,128)S(1)}, u32[]{:S(2)}, u32[]{:S(2)}) collective-permute-start(f32[4,32,512]{2,1,0:T(8,128)S(1)} %get-tuple-element.66), channel_id=1, source_target_pairs={{0,7},{1,6},{2,5},{3,4},{4,3},{5,2},{6,1},{7,0},{8,15},{9,14},{10,... | collective-permute-start | bytes 786440 | tf_op jit(solution)/shard_map/ppermute | solution.py:372
  86.2 26.2 %collective-permute-start.11 = (f32[4,32,512]{2,1,0:T(8,128)S(1)}, f32[4,32,512]{2,1,0:T(8,128)S(1)}, u32[]{:S(2)}, u32[]{:S(2)}) collective-permute-start(f32[4,32,512]{2,1,0:T(8,128)S(1)} %get-tuple-element.63), channel_id=1, source_target_pairs={{0,4},{1,5},{2,6},{3,7},{4,0},{5,1},{6,2},{7,3},{8,12},{9,13},{10,... | collective-permute-start | bytes 786440 | tf_op jit(solution)/shard_map/ppermute | solution.py:372
  86.6 37.1 %collective-permute-start.12 = (f32[4,32,512]{2,1,0:T(8,128)S(1)}, f32[4,32,512]{2,1,0:T(8,128)S(1)}, u32[]{:S(2)}, u32[]{:S(2)}) collective-permute-start(f32[4,32,512]{2,1,0:T(8,128)S(1)} %get-tuple-element.64), channel_id=1, source_target_pairs={{0,5},{1,4},{2,7},{3,6},{4,1},{5,0},{6,3},{7,2},{8,13},{9,12},{10,... | collective-permute-start | bytes 786440 | tf_op jit(solution)/shard_map/ppermute | solution.py:372
  (3 other events, 21.3 us)
where the time goes:
time: 130 us
  waiting for transfers between devices  53.4 us (41%)
  Pallas kernels  42 us (32%)
  starting transfers between devices  33.8 us (26%)
    ppermute x24, waiting for transfers between devices, send(): return lax.ppermute(block, AXES, route)  53.4 us
    ppermute x24, starting transfers between devices, send(): return lax.ppermute(block, AXES, route)  33.8 us
    pallas_call x8, Pallas kernels, smooth_rows(): pl.pallas_call(functools.partial(smooth_body, mask, make_band, rows, cols...  24.4 us
    pallas_call x4, Pallas kernels, expand(): pl.pallas_call(functools.partial(expand_body, masks, local), in_specs=[pl...  6.74 us
    pallas_call x3, Pallas kernels, finish(): pl.pallas_call(functools.partial(finish_body, n_in, starts, top, skip, le...  4.62 us
    pallas_call x4, Pallas kernels, apply_operator(): pl.pallas_call(functools.partial(apply_body, len(stacks), starts, acc is...  3.12 us
    pallas_call x1, Pallas kernels, temporal_operator(): pl.pallas_call(operator_body, in_specs=[vmem] * 2, out_specs=[vmem] * 3,...  3.1 us
  transfers between devices with their start and end apart: 24, of which 7 were waited for; matrix products, arithmetic and copies ran while one was open for 0% of the time, Pallas kernels for 22%

commit v1 on v0

--- a/solution.py
+++ b/solution.py
@@ -337,16 +337,23 @@
     def __init__(self, n_pair, n_quad, rows):
         self.devices = n_pair * n_quad
         self.half = self.devices // 2
-        far = list(range(n_pair // 2, n_pair))
-        middle = len(far) // 2
-        self.far = far[middle:] + far[:middle]
-        near = list(range(n_pair // 4, n_pair // 2))
-        self.near = near
-        self.rest = list(range(n_pair // 4))[::-1]
         groups = rows // SUB
         self.merged = list(range(groups - max(1, groups // 2), groups))
         self.plain = list(range(self.merged[0]))
         self.split = self.merged[0] * SUB
+        far = list(range(n_pair // 2, n_pair))
+        far = far[len(far) // 2 :] + far[: len(far) // 2]
+        near = list(range(n_pair // 4, n_pair // 2))
+        rest = list(range(n_pair // 4))[::-1]
+        cut, middle = len(far) - len(far) // 4, len(near) // 2
+        steps = [("far", mask) for mask in far[:cut]]
+        steps += [("near", mask) for mask in near[:middle]]
+        steps += [("far", mask) for mask in far[cut:]]
+        steps += [("operator", None), ("merge", 0)]
+        steps += [("near", mask) for mask in near[middle:]]
+        steps += [("merge", k) for k in range(1, len(self.merged))]
+        self.steps = steps + [("near", mask) for mask in rest]
+        self.far = far
 
 
 def shards(interferograms, pair_epochs, days):
@@ -371,24 +378,26 @@
         route = [(i, i ^ which) for i in range(plan.devices)]
         return lax.ppermute(block, AXES, route)
 
-    plain, gathered, own = {}, {}, {}
-    for mask in plan.far:
-        blocks = smooth(mask, (plan.split, rows - plan.split))
-        for flip, (first, second) in enumerate(blocks):
-            which = mask * n_quad + flip
-            gathered[which - half] = send(second, which - half)
-            plain[which] = send(first, which)
-    whole, narrow, basis = temporal_operator(pair_epochs, days)
+    plain, gathered, own, arrived = {}, {}, {}, []
     everyone = list(range(half))
-    weights = expand(narrow, everyone, local)
-    arrived = []
-    for k in range(len(plan.merged)):
-        some = apply_operator(weights, [gathered[w] for w in everyone], None, [k * SUB])
-        arrived.append(send(some, half))
-    for mask in plan.near + plan.rest:
-        for flip, (block,) in enumerate(smooth(mask, (rows,))):
-            which = mask * n_quad + flip
-            own[which] = send(block, which)
+    for kind, item in plan.steps:
+        if kind == "far":
+            blocks = smooth(item, (plan.split, rows - plan.split))
+            for flip, (first, second) in enumerate(blocks):
+                which = item * n_quad + flip
+                plain[which] = send(first, which)
+                gathered[which - half] = send(second, which - half)
+        elif kind == "near":
+            for flip, (block,) in enumerate(smooth(item, (rows,))):
+                which = item * n_quad + flip
+                own[which] = send(block, which)
+        elif kind == "operator":
+            whole, narrow, basis = temporal_operator(pair_epochs, days)
+            weights = expand(narrow, everyone, local)
+        else:
+            stacks = [gathered[which] for which in everyone]
+            some = apply_operator(weights, stacks, None, [item * SUB])
+            arrived.append(send(some, half))
     total = None
     starts = [k * SUB for k in plan.plain]
     left = [mask * n_quad + flip for mask in plan.far for flip in range(n_quad)]

time: 130 us -> 133 us (1.023)
  starting transfers between devices: 33.8 us -> 36.7 us
    ppermute x24, starting transfers between devices: 33.8 us -> 36.7 us  [send(): return lax.ppermute(block, AXES, route)]
  transfers between devices with their start and end apart: 24 -> 24, of which waited for: 7 -> 8; matrix products, arithmetic and copies ran while one was open for 0% -> 0% of each run, Pallas kernels for 22% -> 19%
where the time goes in v1:
time: 133 us
  waiting for transfers between devices  53.5 us (40%)
  Pallas kernels  42 us (32%)
  starting transfers between devices  36.7 us (28%)
    ppermute x24, waiting for transfers between devices, send(): return lax.ppermute(block, AXES, route)  53.5 us
    ppermute x24, starting transfers between devices, send(): return lax.ppermute(block, AXES, route)  36.7 us
    pallas_call x8, Pallas kernels, smooth_rows(): pl.pallas_call(functools.partial(smooth_body, mask, make_band, rows, cols...  24.4 us
    pallas_call x4, Pallas kernels, expand(): pl.pallas_call(functools.partial(expand_body, masks, local), in_specs=[pl...  6.74 us
    pallas_call x3, Pallas kernels, finish(): pl.pallas_call(functools.partial(finish_body, n_in, starts, top, skip, le...  4.64 us
    pallas_call x4, Pallas kernels, apply_operator(): pl.pallas_call(functools.partial(apply_body, len(stacks), starts, acc is...  3.11 us
    pallas_call x1, Pallas kernels, temporal_operator(): pl.pallas_call(operator_body, in_specs=[vmem] * 2, out_specs=[vmem] * 3,...  3.1 us
  transfers between devices with their start and end apart: 24, of which 8 were waited for; matrix products, arithmetic and copies ran while one was open for 0% of the time, Pallas kernels for 19%

profile of v1, /device:TPU:0, one launch (start us, length us, event | category | flops | bytes accessed | tf_op | source)
XLA Modules:
  0.0 132.6 jit_solution(8139689980248216747)
XLA Ops:
  0.0 3.0 %shard_map.39 = (f32[4,16,512]{2,1,0:T(8,128)S(1)}, f32[4,16,512]{2,1,0:T(8,128)S(1)}, f32[4,16,512]{2,1,0:T(8,128)S(1)}, f32[4,16,512]{2,1,0:T(8,128)S(1)}, bf1...) custom-call(f32[4,256,1024]{2,1,0:T(8,128)} %x_hbm.15), custom_call_target="tpu_custom_call" | custom-call | flops 1207959552 | bytes 1310720 | tf_op jit(solution)/shard_map/pallas_call | solution.py:196
  3.0 3.0 %shard_map.40 = (f32[4,16,512]{2,1,0:T(8,128)S(1)}, f32[4,16,512]{2,1,0:T(8,128)S(1)}, f32[4,16,512]{2,1,0:T(8,128)S(1)}, f32[4,16,512]{2,1,0:T(8,128)S(1)}, f32[8,128]{1,0:T(8,128)S(1)}) custom-call(f32[4,256,1024]{2,1,0:T(8,128)S(1)} %copy-done, bf16[3,512,256]{2,1,0:T(8,128)(2,1)S(1)} %get-tuple-element.42.refs_0_, f32[8,128]{1,0:T(8,128)S(1)} %get-tuple-element.43.refs_1_), custom_call_target="tpu_custom_call" | custom-call | flops 1207959552 | bytes 1310720 | tf_op jit(solution)/shard_map/pallas_call | solution.py:196
  6.1 3.0 %shard_map.41 = (f32[4,16,512]{2,1,0:T(8,128)S(1)}, f32[4,16,512]{2,1,0:T(8,128)S(1)}, f32[4,16,512]{2,1,0:T(8,128)S(1)}, f32[4,16,512]{2,1,0:T(8,128)S(1)}, f32[8,128]{1,0:T(8,128)S(1)}) custom-call(f32[4,256,1024]{2,1,0:T(8,128)S(1)} %copy-done, bf16[3,512,256]{2,1,0:T(8,128)(2,1)S(1)} %get-tuple-element.42.refs_0_, f32[8,128]{1,0:T(8,128)S(1)} %get-tuple-element.44.refs_1_), custom_call_target="tpu_custom_call" | custom-call | flops 1207959552 | bytes 1310720 | tf_op jit(solution)/shard_map/pallas_call | solution.py:196
  9.1 3.0 %shard_map.42 = (f32[4,32,512]{2,1,0:T(8,128)S(1)}, f32[4,32,512]{2,1,0:T(8,128)S(1)}, f32[8,128]{1,0:T(8,128)S(1)}) custom-call(f32[4,256,1024]{2,1,0:T(8,128)S(1)} %copy-done, bf16[3,512,256]{2,1,0:T(8,128)(2,1)S(1)} %get-tuple-element.42.refs_0_, f32[8,128]{1,0:T(8,128)S(1)} %get-tuple-element.47.refs_1_), custom_call_target="tpu_custom_call" | custom-call | flops 1207959552 | bytes 1310720 | tf_op jit(solution)/shard_map/pallas_call | solution.py:196
  12.1 3.0 %shard_map.43 = (f32[4,16,512]{2,1,0:T(8,128)S(1)}, f32[4,16,512]{2,1,0:T(8,128)S(1)}, f32[4,16,512]{2,1,0:T(8,128)S(1)}, f32[4,16,512]{2,1,0:T(8,128)S(1)}, f32[8,128]{1,0:T(8,128)S(1)}) custom-call(f32[4,256,1024]{2,1,0:T(8,128)S(1)} %copy-done, bf16[3,512,256]{2,1,0:T(8,128)(2,1)S(1)} %get-tuple-element.42.refs_0_, f32[8,128]{1,0:T(8,128)S(1)} %get-tuple-element.48.refs_1_), custom_call_target="tpu_custom_call" | custom-call | flops 1207959552 | bytes 1310720 | tf_op jit(solution)/shard_map/pallas_call | solution.py:196
  15.1 5.1 %collective-permute-start.22 = (f32[4,16,512]{2,1,0:T(8,128)S(1)}, f32[4,16,512]{2,1,0:T(8,128)S(1)}, u32[]{:S(2)}, u32[]{:S(2)}) collective-permute-start(f32[4,16,512]{2,1,0:T(8,128)S(1)} %get-tuple-element.73), channel_id=1, source_target_pairs={{0,10},{1,11},{2,8},{3,9},{4,14},{5,15},{6,12},{7,13},{8,2},{9,3},... | collective-permute-start | bytes 393224 | tf_op jit(solution)/shard_map/ppermute | solution.py:379
  20.2 2.0 %collective-permute-start.20 = (f32[4,16,512]{2,1,0:T(8,128)S(1)}, f32[4,16,512]{2,1,0:T(8,128)S(1)}, u32[]{:S(2)}, u32[]{:S(2)}) collective-permute-start(f32[4,16,512]{2,1,0:T(8,128)S(1)} %get-tuple-element.71), channel_id=1, source_target_pairs={{0,8},{1,9},{2,10},{3,11},{4,12},{5,13},{6,14},{7,15},{8,0},{9,1},... | collective-permute-start | bytes 393224 | tf_op jit(solution)/shard_map/ppermute | solution.py:379
  22.8 4.6 %collective-permute-start.18 = (f32[4,16,512]{2,1,0:T(8,128)S(1)}, f32[4,16,512]{2,1,0:T(8,128)S(1)}, u32[]{:S(2)}, u32[]{:S(2)}) collective-permute-start(f32[4,16,512]{2,1,0:T(8,128)S(1)} %get-tuple-element.69), channel_id=1, source_target_pairs={{0,14},{1,15},{2,12},{3,13},{4,10},{5,11},{6,8},{7,9},{8,6},{9,7},... | collective-permute-start | bytes 393224 | tf_op jit(solution)/shard_map/ppermute | solution.py:379
  27.4 11.2 %collective-permute-done.22.refs_6_ = f32[4,16,512]{2,1,0:T(8,128)S(1)} collective-permute-done((f32[4,16,512]{2,1,0:T(8,128)S(1)}, f32[4,16,512]{2,1,0:T(8,128)S(1)}, u32[]{:S(2)}, u32[]{:S(2)}) %collective-permute-start.22) | collective-permute-done | bytes 131104 | tf_op jit(solution)/shard_map/ppermute | solution.py:379
  38.6 3.2 %collective-permute-start.19 = (f32[4,16,512]{2,1,0:T(8,128)S(1)}, f32[4,16,512]{2,1,0:T(8,128)S(1)}, u32[]{:S(2)}, u32[]{:S(2)}) collective-permute-start(f32[4,16,512]{2,1,0:T(8,128)S(1)} %get-tuple-element.70), channel_id=1, source_target_pairs={{0,15},{1,14},{2,13},{3,12},{4,11},{5,10},{6,9},{7,8},{8,7},{9,6},... | collective-permute-start | bytes 393224 | tf_op jit(solution)/shard_map/ppermute | solution.py:379
  41.8 2.1 %collective-permute-start.16 = (f32[4,16,512]{2,1,0:T(8,128)S(1)}, f32[4,16,512]{2,1,0:T(8,128)S(1)}, u32[]{:S(2)}, u32[]{:S(2)}) collective-permute-start(f32[4,16,512]{2,1,0:T(8,128)S(1)} %get-tuple-element.67), channel_id=1, source_target_pairs={{0,12},{1,13},{2,14},{3,15},{4,8},{5,9},{6,10},{7,11},{8,4},{9,5},... | collective-permute-start | bytes 393224 | tf_op jit(solution)/shard_map/ppermute | solution.py:379
  43.9 6.2 %collective-permute-done.20.refs_4_ = f32[4,16,512]{2,1,0:T(8,128)S(1)} collective-permute-done((f32[4,16,512]{2,1,0:T(8,128)S(1)}, f32[4,16,512]{2,1,0:T(8,128)S(1)}, u32[]{:S(2)}, u32[]{:S(2)}) %collective-permute-start.20) | collective-permute-done | bytes 131104 | tf_op jit(solution)/shard_map/ppermute | solution.py:379
  52.6 3.0 %shard_map.46 = (f32[4,32,512]{2,1,0:T(8,128)S(1)}, f32[4,32,512]{2,1,0:T(8,128)S(1)}, f32[8,128]{1,0:T(8,128)S(1)}) custom-call(f32[4,256,1024]{2,1,0:T(8,128)S(1)} %copy-done, bf16[3,512,256]{2,1,0:T(8,128)(2,1)S(1)} %get-tuple-element.42.refs_0_, f32[8,128]{1,0:T(8,128)S(1)} %get-tuple-element.56.refs_1_), custom_call_target="tpu_custom_call" | custom-call | flops 1207959552 | bytes 1310720 | tf_op jit(solution)/shard_map/pallas_call | solution.py:196
  55.8 2.4 %collective-permute-start.5 = (f32[4,16,512]{2,1,0:T(8,128)S(1)}, f32[4,16,512]{2,1,0:T(8,128)S(1)}, u32[]{:S(2)}, u32[]{:S(2)}) collective-permute-start(f32[4,16,512]{2,1,0:T(8,128)S(1)} %get-tuple-element.53), channel_id=1, source_target_pairs={{0,6},{1,7},{2,4},{3,5},{4,2},{5,3},{6,0},{7,1},{8,14},{9,15},{10,... | collective-permute-start | bytes 393224 | tf_op jit(solution)/shard_map/ppermute | solution.py:379
  58.2 2.3 %collective-permute-start.6 = (f32[4,16,512]{2,1,0:T(8,128)S(1)}, f32[4,16,512]{2,1,0:T(8,128)S(1)}, u32[]{:S(2)}, u32[]{:S(2)}) collective-permute-start(f32[4,16,512]{2,1,0:T(8,128)S(1)} %get-tuple-element.54), channel_id=1, source_target_pairs={{0,7},{1,6},{2,5},{3,4},{4,3},{5,2},{6,1},{7,0},{8,15},{9,14},{10,... | collective-permute-start | bytes 393224 | tf_op jit(solution)/shard_map/ppermute | solution.py:379
  61.0 3.0 %shard_map.47 = (f32[4,32,512]{2,1,0:T(8,128)S(1)}, f32[4,32,512]{2,1,0:T(8,128)S(1)}, f32[8,128]{1,0:T(8,128)S(1)}) custom-call(f32[4,256,1024]{2,1,0:T(8,128)S(1)} %copy-done, bf16[3,512,256]{2,1,0:T(8,128)(2,1)S(1)} %get-tuple-element.42.refs_0_, f32[8,128]{1,0:T(8,128)S(1)} %get-tuple-element.57.refs_1_), custom_call_target="tpu_custom_call" | custom-call | flops 1207959552 | bytes 1310720 | tf_op jit(solution)/shard_map/pallas_call | solution.py:196
  65.4 3.4 %shard_map.48 = (f32[4,32,512]{2,1,0:T(8,128)S(1)}, f32[4,32,512]{2,1,0:T(8,128)S(1)}, f32[8,128]{1,0:T(8,128)}) custom-call(f32[4,256,1024]{2,1,0:T(8,128)S(1)} %copy-done, bf16[3,512,256]{2,1,0:T(8,128)(2,1)S(1)} %get-tuple-element.42.refs_0_, f32[8,128]{1,0:T(8,128)S(1)} %get-tuple-element.58.refs_1_), custom_call_target="tpu_custom_call" | custom-call | flops 1207959552 | bytes 1310720 | tf_op jit(solution)/shard_map/pallas_call | solution.py:196
  72.5 2.4 %collective-permute-start.17 = (f32[4,16,512]{2,1,0:T(8,128)S(1)}, f32[4,16,512]{2,1,0:T(8,128)S(1)}, u32[]{:S(2)}, u32[]{:S(2)}) collective-permute-start(f32[4,16,512]{2,1,0:T(8,128)S(1)} %get-tuple-element.68), channel_id=1, source_target_pairs={{0,13},{1,12},{2,15},{3,14},{4,9},{5,8},{6,11},{7,10},{8,5},{9,4},... | collective-permute-start | bytes 393224 | tf_op jit(solution)/shard_map/ppermute | solution.py:379
  74.9 3.1 %operator.1 = (f32[32,64]{1,0:T(8,128)S(1)}, f32[28,64]{1,0:T(8,128)S(1)}, f32[32,28]{1,0:T(8,128)S(1)}) custom-call(s32[2,64]{1,0:T(2,128)S(1)} %copy-done.1, s32[1,32]{1,0:T(1,128)S(1)} %bitcast.1), custom_call_target="tpu_custom_call" | custom-call | tf_op jit(solution)/shard_map/operator/pallas_call | solution.py:81
  80.1 3.4 %collective-permute-done.17.refs_1_ = f32[4,16,512]{2,1,0:T(8,128)S(1)} collective-permute-done((f32[4,16,512]{2,1,0:T(8,128)S(1)}, f32[4,16,512]{2,1,0:T(8,128)S(1)}, u32[]{:S(2)}, u32[]{:S(2)}) %collective-permute-start.17) | collective-permute-done | bytes 131104 | tf_op jit(solution)/shard_map/ppermute | solution.py:379
  84.1 3.0 %collective-permute-start.7 = (f32[28,8,512]{2,1,0:T(8,128)S(1)}, f32[28,8,512]{2,1,0:T(8,128)S(1)}, u32[]{:S(2)}, u32[]{:S(2)}) collective-permute-start(f32[28,8,512]{2,1,0:T(8,128)S(1)} %shard_map.44), channel_id=1, source_target_pairs={{0,8},{1,9},{2,10},{3,11},{4,12},{5,13},{6,14},{7,15},{8,0},{9,1},... | collective-permute-start | bytes 1376264 | tf_op jit(solution)/shard_map/ppermute | solution.py:379
  96.4 13.4 %collective-permute-done.14.refs_7_ = f32[4,32,512]{2,1,0:T(8,128)S(1)} collective-permute-done((f32[4,32,512]{2,1,0:T(8,128)S(1)}, f32[4,32,512]{2,1,0:T(8,128)S(1)}, u32[]{:S(2)}, u32[]{:S(2)}) %collective-permute-start.14) | collective-permute-done | bytes 262176 | tf_op jit(solution)/shard_map/ppermute | solution.py:379
  109.8 5.6 %collective-permute-done.11.refs_4_ = f32[4,32,512]{2,1,0:T(8,128)S(1)} collective-permute-done((f32[4,32,512]{2,1,0:T(8,128)S(1)}, f32[4,32,512]{2,1,0:T(8,128)S(1)}, u32[]{:S(2)}, u32[]{:S(2)}) %collective-permute-start.11) | collective-permute-done | bytes 262176 | tf_op jit(solution)/shard_map/ppermute | solution.py:379
  115.4 11.3 %collective-permute-done.12.refs_5_ = f32[4,32,512]{2,1,0:T(8,128)S(1)} collective-permute-done((f32[4,32,512]{2,1,0:T(8,128)S(1)}, f32[4,32,512]{2,1,0:T(8,128)S(1)}, u32[]{:S(2)}, u32[]{:S(2)}) %collective-permute-start.12) | collective-permute-done | bytes 262176 | tf_op jit(solution)/shard_map/ppermute | solution.py:379
  (50 shorter events, 26.4 us)
Async XLA Ops:
  15.1 23.5 %collective-permute-start.22 = (f32[4,16,512]{2,1,0:T(8,128)S(1)}, f32[4,16,512]{2,1,0:T(8,128)S(1)}, u32[]{:S(2)}, u32[]{:S(2)}) collective-permute-start(f32[4,16,512]{2,1,0:T(8,128)S(1)} %get-tuple-element.73), channel_id=1, source_target_pairs={{0,10},{1,11},{2,8},{3,9},{4,14},{5,15},{6,12},{7,13},{8,2},{9,3},... | collective-permute-start | bytes 393224 | tf_op jit(solution)/shard_map/ppermute | solution.py:379
  20.2 21.6 %collective-permute-start.23 = (f32[4,16,512]{2,1,0:T(8,128)S(1)}, f32[4,16,512]{2,1,0:T(8,128)S(1)}, u32[]{:S(2)}, u32[]{:S(2)}) collective-permute-start(f32[4,16,512]{2,1,0:T(8,128)S(1)} %get-tuple-element.74), channel_id=1, source_target_pairs={{0,11},{1,10},{2,9},{3,8},{4,15},{5,14},{6,13},{7,12},{8,3},{9,2},... | collective-permute-start | bytes 393224 | tf_op jit(solution)/shard_map/ppermute | solution.py:379
  20.2 29.9 %collective-permute-start.20 = (f32[4,16,512]{2,1,0:T(8,128)S(1)}, f32[4,16,512]{2,1,0:T(8,128)S(1)}, u32[]{:S(2)}, u32[]{:S(2)}) collective-permute-start(f32[4,16,512]{2,1,0:T(8,128)S(1)} %get-tuple-element.71), channel_id=1, source_target_pairs={{0,8},{1,9},{2,10},{3,11},{4,12},{5,13},{6,14},{7,15},{8,0},{9,1},... | collective-permute-start | bytes 393224 | tf_op jit(solution)/shard_map/ppermute | solution.py:379
  22.2 28.5 %collective-permute-start.21 = (f32[4,16,512]{2,1,0:T(8,128)S(1)}, f32[4,16,512]{2,1,0:T(8,128)S(1)}, u32[]{:S(2)}, u32[]{:S(2)}) collective-permute-start(f32[4,16,512]{2,1,0:T(8,128)S(1)} %get-tuple-element.72), channel_id=1, source_target_pairs={{0,9},{1,8},{2,11},{3,10},{4,13},{5,12},{6,15},{7,14},{8,1},{9,0},... | collective-permute-start | bytes 393224 | tf_op jit(solution)/shard_map/ppermute | solution.py:379
  22.8 32.8 %collective-permute-start.18 = (f32[4,16,512]{2,1,0:T(8,128)S(1)}, f32[4,16,512]{2,1,0:T(8,128)S(1)}, u32[]{:S(2)}, u32[]{:S(2)}) collective-permute-start(f32[4,16,512]{2,1,0:T(8,128)S(1)} %get-tuple-element.69), channel_id=1, source_target_pairs={{0,14},{1,15},{2,12},{3,13},{4,10},{5,11},{6,8},{7,9},{8,6},{9,7},... | collective-permute-start | bytes 393224 | tf_op jit(solution)/shard_map/ppermute | solution.py:379
  38.6 17.2 %collective-permute-start.19 = (f32[4,16,512]{2,1,0:T(8,128)S(1)}, f32[4,16,512]{2,1,0:T(8,128)S(1)}, u32[]{:S(2)}, u32[]{:S(2)}) collective-permute-start(f32[4,16,512]{2,1,0:T(8,128)S(1)} %get-tuple-element.70), channel_id=1, source_target_pairs={{0,15},{1,14},{2,13},{3,12},{4,11},{5,10},{6,9},{7,8},{8,7},{9,6},... | collective-permute-start | bytes 393224 | tf_op jit(solution)/shard_map/ppermute | solution.py:379
  41.8 16.4 %collective-permute-start.16 = (f32[4,16,512]{2,1,0:T(8,128)S(1)}, f32[4,16,512]{2,1,0:T(8,128)S(1)}, u32[]{:S(2)}, u32[]{:S(2)}) collective-permute-start(f32[4,16,512]{2,1,0:T(8,128)S(1)} %get-tuple-element.67), channel_id=1, source_target_pairs={{0,12},{1,13},{2,14},{3,15},{4,8},{5,9},{6,10},{7,11},{8,4},{9,5},... | collective-permute-start | bytes 393224 | tf_op jit(solution)/shard_map/ppermute | solution.py:379
  50.1 10.4 %collective-permute-start.1 = (f32[4,16,512]{2,1,0:T(8,128)S(1)}, f32[4,16,512]{2,1,0:T(8,128)S(1)}, u32[]{:S(2)}, u32[]{:S(2)}) collective-permute-start(f32[4,16,512]{2,1,0:T(8,128)S(1)} %get-tuple-element.49), channel_id=1, source_target_pairs={{0,2},{1,3},{2,0},{3,1},{4,6},{5,7},{6,4},{7,5},{8,10},{9,11},{10,... | collective-permute-start | bytes 393224 | tf_op jit(solution)/shard_map/ppermute | solution.py:379
  50.7 13.2 %collective-permute-start.2 = (f32[4,16,512]{2,1,0:T(8,128)S(1)}, f32[4,16,512]{2,1,0:T(8,128)S(1)}, u32[]{:S(2)}, u32[]{:S(2)}) collective-permute-start(f32[4,16,512]{2,1,0:T(8,128)S(1)} %get-tuple-element.50), channel_id=1, source_target_pairs={{0,3},{1,2},{2,1},{3,0},{4,7},{5,6},{6,5},{7,4},{8,11},{9,10},{10,... | collective-permute-start | bytes 393224 | tf_op jit(solution)/shard_map/ppermute | solution.py:379
  55.6 13.3 %collective-permute-start = (f32[4,16,512]{2,1,0:T(8,128)S(1)}, f32[4,16,512]{2,1,0:T(8,128)S(1)}, u32[]{:S(2)}, u32[]{:S(2)}) collective-permute-start(f32[4,16,512]{2,1,0:T(8,128)S(1)} %get-tuple-element.46), channel_id=1, source_target_pairs={{0,1},{1,0},{2,3},{3,2},{4,5},{5,4},{6,7},{7,6},{8,9},{9,8},{10,11... | collective-permute-start | bytes 393224 | tf_op jit(solution)/shard_map/ppermute | solution.py:379
  55.8 13.4 %collective-permute-start.5 = (f32[4,16,512]{2,1,0:T(8,128)S(1)}, f32[4,16,512]{2,1,0:T(8,128)S(1)}, u32[]{:S(2)}, u32[]{:S(2)}) collective-permute-start(f32[4,16,512]{2,1,0:T(8,128)S(1)} %get-tuple-element.53), channel_id=1, source_target_pairs={{0,6},{1,7},{2,4},{3,5},{4,2},{5,3},{6,0},{7,1},{8,14},{9,15},{10,... | collective-permute-start | bytes 393224 | tf_op jit(solution)/shard_map/ppermute | solution.py:379
  58.2 12.4 %collective-permute-start.6 = (f32[4,16,512]{2,1,0:T(8,128)S(1)}, f32[4,16,512]{2,1,0:T(8,128)S(1)}, u32[]{:S(2)}, u32[]{:S(2)}) collective-permute-start(f32[4,16,512]{2,1,0:T(8,128)S(1)} %get-tuple-element.54), channel_id=1, source_target_pairs={{0,7},{1,6},{2,5},{3,4},{4,3},{5,2},{6,1},{7,0},{8,15},{9,14},{10,... | collective-permute-start | bytes 393224 | tf_op jit(solution)/shard_map/ppermute | solution.py:379
  60.5 10.6 %collective-permute-start.3 = (f32[4,16,512]{2,1,0:T(8,128)S(1)}, f32[4,16,512]{2,1,0:T(8,128)S(1)}, u32[]{:S(2)}, u32[]{:S(2)}) collective-permute-start(f32[4,16,512]{2,1,0:T(8,128)S(1)} %get-tuple-element.51), channel_id=1, source_target_pairs={{0,4},{1,5},{2,6},{3,7},{4,0},{5,1},{6,2},{7,3},{8,12},{9,13},{10,... | collective-permute-start | bytes 393224 | tf_op jit(solution)/shard_map/ppermute | solution.py:379
  63.9 8.6 %collective-permute-start.4 = (f32[4,16,512]{2,1,0:T(8,128)S(1)}, f32[4,16,512]{2,1,0:T(8,128)S(1)}, u32[]{:S(2)}, u32[]{:S(2)}) collective-permute-start(f32[4,16,512]{2,1,0:T(8,128)S(1)} %get-tuple-element.52), channel_id=1, source_target_pairs={{0,5},{1,4},{2,7},{3,6},{4,1},{5,0},{6,3},{7,2},{8,13},{9,12},{10,... | collective-permute-start | bytes 393224 | tf_op jit(solution)/shard_map/ppermute | solution.py:379
  68.9 15.3 %collective-permute-start.8 = (f32[4,32,512]{2,1,0:T(8,128)S(1)}, f32[4,32,512]{2,1,0:T(8,128)S(1)}, u32[]{:S(2)}, u32[]{:S(2)}) collective-permute-start(f32[4,32,512]{2,1,0:T(8,128)S(1)} %get-tuple-element.60), channel_id=1, source_target_pairs={{0,1},{1,0},{2,3},{3,2},{4,5},{5,4},{6,7},{7,6},{8,9},{9,8},{10,11... | collective-permute-start | bytes 786440 | tf_op jit(solution)/shard_map/ppermute | solution.py:379
  69.2 17.9 %collective-permute-start.10 = (f32[4,32,512]{2,1,0:T(8,128)S(1)}, f32[4,32,512]{2,1,0:T(8,128)S(1)}, u32[]{:S(2)}, u32[]{:S(2)}) collective-permute-start(f32[4,32,512]{2,1,0:T(8,128)S(1)} %get-tuple-element.62), channel_id=1, source_target_pairs={{0,3},{1,2},{2,1},{3,0},{4,7},{5,6},{6,5},{7,4},{8,11},{9,10},{10,... | collective-permute-start | bytes 786440 | tf_op jit(solution)/shard_map/ppermute | solution.py:379
  70.6 18.5 %collective-permute-start.9 = (f32[4,32,512]{2,1,0:T(8,128)S(1)}, f32[4,32,512]{2,1,0:T(8,128)S(1)}, u32[]{:S(2)}, u32[]{:S(2)}) collective-permute-start(f32[4,32,512]{2,1,0:T(8,128)S(1)} %get-tuple-element.61), channel_id=1, source_target_pairs={{0,2},{1,3},{2,0},{3,1},{4,6},{5,7},{6,4},{7,5},{8,10},{9,11},{10,... | collective-permute-start | bytes 786440 | tf_op jit(solution)/shard_map/ppermute | solution.py:379
  71.1 18.4 %collective-permute-start.13 = (f32[4,32,512]{2,1,0:T(8,128)S(1)}, f32[4,32,512]{2,1,0:T(8,128)S(1)}, u32[]{:S(2)}, u32[]{:S(2)}) collective-permute-start(f32[4,32,512]{2,1,0:T(8,128)S(1)} %get-tuple-element.65), channel_id=1, source_target_pairs={{0,6},{1,7},{2,4},{3,5},{4,2},{5,3},{6,0},{7,1},{8,14},{9,15},{10,... | collective-permute-start | bytes 786440 | tf_op jit(solution)/shard_map/ppermute | solution.py:379
  72.5 11.0 %collective-permute-start.17 = (f32[4,16,512]{2,1,0:T(8,128)S(1)}, f32[4,16,512]{2,1,0:T(8,128)S(1)}, u32[]{:S(2)}, u32[]{:S(2)}) collective-permute-start(f32[4,16,512]{2,1,0:T(8,128)S(1)} %get-tuple-element.68), channel_id=1, source_target_pairs={{0,13},{1,12},{2,15},{3,14},{4,9},{5,8},{6,11},{7,10},{8,5},{9,4},... | collective-permute-start | bytes 393224 | tf_op jit(solution)/shard_map/ppermute | solution.py:379
  83.6 46.0 %collective-permute-start.15 = (f32[28,8,512]{2,1,0:T(8,128)S(1)}, f32[28,8,512]{2,1,0:T(8,128)S(1)}, u32[]{:S(2)}, u32[]{:S(2)}) collective-permute-start(f32[28,8,512]{2,1,0:T(8,128)S(1)} %shard_map.50), channel_id=1, source_target_pairs={{0,8},{1,9},{2,10},{3,11},{4,12},{5,13},{6,14},{7,15},{8,0},{9,1},... | collective-permute-start | bytes 1376264 | tf_op jit(solution)/shard_map/ppermute | solution.py:379
  84.1 46.9 %collective-permute-start.7 = (f32[28,8,512]{2,1,0:T(8,128)S(1)}, f32[28,8,512]{2,1,0:T(8,128)S(1)}, u32[]{:S(2)}, u32[]{:S(2)}) collective-permute-start(f32[28,8,512]{2,1,0:T(8,128)S(1)} %shard_map.44), channel_id=1, source_target_pairs={{0,8},{1,9},{2,10},{3,11},{4,12},{5,13},{6,14},{7,15},{8,0},{9,1},... | collective-permute-start | bytes 1376264 | tf_op jit(solution)/shard_map/ppermute | solution.py:379
  87.1 22.7 %collective-permute-start.14 = (f32[4,32,512]{2,1,0:T(8,128)S(1)}, f32[4,32,512]{2,1,0:T(8,128)S(1)}, u32[]{:S(2)}, u32[]{:S(2)}) collective-permute-start(f32[4,32,512]{2,1,0:T(8,128)S(1)} %get-tuple-element.66), channel_id=1, source_target_pairs={{0,7},{1,6},{2,5},{3,4},{4,3},{5,2},{6,1},{7,0},{8,15},{9,14},{10,... | collective-permute-start | bytes 786440 | tf_op jit(solution)/shard_map/ppermute | solution.py:379
  89.1 26.3 %collective-permute-start.11 = (f32[4,32,512]{2,1,0:T(8,128)S(1)}, f32[4,32,512]{2,1,0:T(8,128)S(1)}, u32[]{:S(2)}, u32[]{:S(2)}) collective-permute-start(f32[4,32,512]{2,1,0:T(8,128)S(1)} %get-tuple-element.63), channel_id=1, source_target_pairs={{0,4},{1,5},{2,6},{3,7},{4,0},{5,1},{6,2},{7,3},{8,12},{9,13},{10,... | collective-permute-start | bytes 786440 | tf_op jit(solution)/shard_map/ppermute | solution.py:379
  89.5 37.2 %collective-permute-start.12 = (f32[4,32,512]{2,1,0:T(8,128)S(1)}, f32[4,32,512]{2,1,0:T(8,128)S(1)}, u32[]{:S(2)}, u32[]{:S(2)}) collective-permute-start(f32[4,32,512]{2,1,0:T(8,128)S(1)} %get-tuple-element.64), channel_id=1, source_target_pairs={{0,5},{1,4},{2,7},{3,6},{4,1},{5,0},{6,3},{7,2},{8,13},{9,12},{10,... | collective-permute-start | bytes 786440 | tf_op jit(solution)/shard_map/ppermute | solution.py:379
  (3 other events, 22.1 us)
